TPU v7x, 512 devices: a whole 4x8x8 slice. The times are simulated.
512 devices in a mesh: axial: 64 (over x, z, core), radial: 8 (over y).
Axes of the slice: x: 4, y: 8, z: 8, core: 2. Of those that a mesh axis runs over, the one named last changes fastest.
Arguments:
- state_start: float32 [5, 640, 128, 128], P(None, 'axial', 'radial'), may hold values from -6 to 6
- forcing: float32 [640, 128, 128], P('axial', 'radial'), may hold values from -6 to 6
- signal: float32 [8], replicated, may hold values from -1 to 1
- mixing: float32 [2, 5, 5], replicated, may hold values from -0.4 to 0.4
- panel_cell: int32 [64, 8, 64, 4], P('axial', 'radial'), may hold values from -1 to 20479, as said below
- amplitude: float32 [64, 8, 64, 4, 512], P('axial', 'radial'), may hold values from -0.015625 to 0.015625
- delay: float32 [64, 8, 64, 4, 512], P('axial', 'radial'), may hold values from 0 to 8
- observer_list: int32 [512], replicated, may hold values from 0 to 511, each once
Outputs:
- final_state: float32 [5, 640, 128, 128], P(None, 'axial', 'radial')
- spectra: float32 [2, 4, 512], P(None, None, ('axial', 'radial'))
- adjoint_state: float32 [5, 640, 128, 128], P(None, 'axial', 'radial')
- forcing_grad: float32 [640, 128, 128], P('axial', 'radial')
Inputs may be any that keep to these rules, and one draw needn't show every extreme that they name: `panel_cell`: each entry is a cell index of the sending tile, of 20480 cells, or -1 for an empty slot; the live slots of one tile and owner come first; one owner in each draw receives 4 live slots from every tile, and the largest cell index is reached.
All inputs are finite; a program needn't handle non-finite values.
Results may differ from a plain program's by a relative error of at most 0.0003.
Values sent between devices are 32-bit elements; how exact they have to be, the bound alone decides.
A program may use at most 128 MiB of HBM per device.

v0:
```python
import math
import jax
import jax.numpy as jnp
from jax import lax
from jax.sharding import PartitionSpec as P

STEPS = 8
FREQ = 4
deriv_coef = (5.0 / 6.0, -5.0 / 21.0, 5.0 / 84.0, -5.0 / 504.0, 1.0 / 1260.0)
filter_coef = tuple(
    ((-1.0) ** abs(offset) * math.comb(10, 5 + offset) / 1024.0 for offset in range(-5, 6))
)
damping = 0.2
highest = lax.Precision.HIGHEST


def extended(block, sides, width):
    for axis, dim in sides:
        count = lax.axis_size(axis)
        forward = [(i, i + 1) for i in range(count - 1)]
        backward = [(target, source) for source, target in forward]
        low = lax.ppermute(
            lax.slice_in_dim(block, block.shape[dim] - width, None, axis=dim), axis, forward
        )
        high = lax.ppermute(lax.slice_in_dim(block, 0, width, axis=dim), axis, backward)
        block = jnp.concatenate([low, block, high], axis=dim)
    return block


def advance(padded, mixing, adjoint):
    span_x = padded.shape[1] - 10
    span_r = padded.shape[2] - 10
    count = padded.shape[0]

    def along_x(offset):
        return padded[:, 5 + offset : 5 + offset + span_x, 5 : 5 + span_r, :]

    def along_r(offset):
        return padded[:, 5 : 5 + span_x, 5 + offset : 5 + offset + span_r, :]

    centre = along_x(0)
    deriv_x = sum(
        (deriv_coef[order] * (along_x(order + 1) - along_x(-order - 1)) for order in range(5))
    )
    deriv_r = sum(
        (deriv_coef[order] * (along_r(order + 1) - along_r(-order - 1)) for order in range(5))
    )
    smooth = sum(
        (filter_coef[offset + 5] * (along_x(offset) + along_r(offset)) for offset in range(-5, 6))
    )
    factor = 1.0 if adjoint else -1.0
    outputs = []
    for target in range(count):
        term = centre[target] - damping * smooth[target]
        for source in range(count):
            if adjoint:
                coef_x = mixing[0, source, target]
                coef_r = mixing[1, source, target]
            else:
                coef_x = mixing[0, target, source]
                coef_r = mixing[1, target, source]
            term = term + factor * (coef_x * deriv_x[source] + coef_r * deriv_r[source])
        outputs.append(term)
    return jnp.stack(outputs)


def frequencies():
    return 2.0 * jnp.pi * (jnp.arange(FREQ, dtype=jnp.float32) + 1.0) / STEPS


def time_tables():
    levels = jnp.arange(STEPS, dtype=jnp.float32)
    phase = levels[:, None] * frequencies()[None, :]
    return (jnp.cos(phase), jnp.sin(phase))


def panel_kernels(amp, lag):
    phase = frequencies()[None, :, None] * lag[:, None, :]
    return (amp[:, None, :] * jnp.cos(phase), -amp[:, None, :] * jnp.sin(phase))


def partial_spectra(panels, kern_re, kern_im, cos_t, sin_t):
    coef_re = jnp.dot(panels, cos_t, precision=highest)
    coef_im = -jnp.dot(panels, sin_t, precision=highest)
    spec_re = jnp.einsum("pfo,pf->fo", kern_re, coef_re, precision=highest) - jnp.einsum(
        "pfo,pf->fo", kern_im, coef_im, precision=highest
    )
    spec_im = jnp.einsum("pfo,pf->fo", kern_re, coef_im, precision=highest) + jnp.einsum(
        "pfo,pf->fo", kern_im, coef_re, precision=highest
    )
    return jnp.stack([spec_re, spec_im])


def panel_sources(spectra, kern_re, kern_im, cos_t, sin_t):
    back_re = jnp.einsum("pfo,fo->pf", kern_re, spectra[0], precision=highest) + jnp.einsum(
        "pfo,fo->pf", kern_im, spectra[1], precision=highest
    )
    back_im = jnp.einsum("pfo,fo->pf", kern_im, spectra[0], precision=highest) - jnp.einsum(
        "pfo,fo->pf", kern_re, spectra[1], precision=highest
    )
    return 2.0 * (
        jnp.dot(back_re, cos_t.T, precision=highest) + jnp.dot(back_im, sin_t.T, precision=highest)
    )


def on_device(state_start, forcing, signal, mixing, panel_cell, amplitude, delay, observer_list):
    slots = panel_cell[0, 0]
    cell_total = forcing.shape[0] * forcing.shape[1] * forcing.shape[2]
    live = slots >= 0
    targets = jnp.where(live, slots, cell_total)
    clipped = jnp.minimum(targets, cell_total - 1)
    state = state_start
    records = []
    for level in range(STEPS):
        padded = extended(state, (("axial", 1), ("radial", 2)), 5)
        state = advance(padded, mixing, False).at[4].add(signal[level] * forcing)
        records.append(jnp.where(live, jnp.take(state[4].reshape(-1), clipped), 0.0))
    stacked = jnp.stack(records, axis=-1)
    received = lax.all_to_all(stacked, "axial", split_axis=0, concat_axis=0, tiled=True)
    observers = observer_list.shape[0]
    chosen_amp = jnp.take(amplitude[0, 0], observer_list, axis=2).reshape(-1, observers)
    chosen_lag = jnp.take(delay[0, 0], observer_list, axis=2).reshape(-1, observers)
    kern_re, kern_im = panel_kernels(chosen_amp, chosen_lag)
    cos_t, sin_t = time_tables()
    partial_sum = partial_spectra(received.reshape(-1, STEPS), kern_re, kern_im, cos_t, sin_t)
    share = observers // lax.axis_size(("axial", "radial"))
    total = lax.psum(partial_sum, ("axial", "radial"))
    mine = lax.dynamic_slice_in_dim(total, lax.axis_index(("axial", "radial")) * share, share, 2)
    sources = panel_sources(total, kern_re, kern_im, cos_t, sin_t).reshape(received.shape)
    returned = lax.all_to_all(sources, "axial", split_axis=0, concat_axis=0, tiled=True)
    flat_targets = targets.reshape(-1)
    adjoint = jnp.zeros_like(state_start)
    gradient = jnp.zeros_like(forcing)
    for level in reversed(range(STEPS)):
        spread = (
            jnp.zeros((cell_total,), jnp.float32)
            .at[flat_targets]
            .add(returned[:, :, level].reshape(-1), mode="drop")
        )
        carried = adjoint.at[4].add(spread.reshape(forcing.shape))
        gradient = gradient + signal[level] * carried[4]
        padded = extended(carried, (("axial", 1), ("radial", 2)), 5)
        adjoint = advance(padded, mixing, True)
    return (state, mine, adjoint, gradient)


def solution(mesh):
    return jax.shard_map(
        on_device,
        mesh=mesh,
        in_specs=(
            P(None, "axial", "radial", None),
            P("axial", "radial", None),
            P(),
            P(),
            P("axial", "radial", None, None),
            P("axial", "radial", None, None, None),
            P("axial", "radial", None, None, None),
            P(),
        ),
        out_specs=(
            P(None, "axial", "radial", None),
            P(None, None, ("axial", "radial")),
            P(None, "axial", "radial", None),
            P("axial", "radial", None),
        ),
        check_vma=False,
    )
```

profile of v0, /device:TPU:64, one launch (start us, length us, event | category | flops | bytes accessed | tf_op | source)
XLA Modules:
  0.0 1145.9 jit_solution(15424200699040122054)
XLA Ops:
  19.7 7.2 collective-permute-done.3
  29.7 6.4 constant_dynamic-update-slice_fusion.11
  36.1 6.3 constant_dynamic-update-slice_fusion.10
  42.4 6.4 constant_dynamic-update-slice_fusion.9
  77.0 7.1 collective-permute-done.6
  90.4 6.4 constant_dynamic-update-slice_fusion.16
  96.7 6.3 constant_dynamic-update-slice_fusion.15
  103.1 6.5 constant_dynamic-update-slice_fusion.14
  148.3 6.4 constant_dynamic-update-slice_fusion.21
  154.7 6.3 constant_dynamic-update-slice_fusion.20
  161.0 6.4 constant_dynamic-update-slice_fusion.19
  214.7 6.4 constant_dynamic-update-slice_fusion.26
  221.1 6.3 constant_dynamic-update-slice_fusion.25
  227.4 6.4 constant_dynamic-update-slice_fusion.24
  281.9 6.4 constant_dynamic-update-slice_fusion.31
  288.3 6.3 constant_dynamic-update-slice_fusion.30
  294.6 6.4 constant_dynamic-update-slice_fusion.29
  340.7 6.4 constant_dynamic-update-slice_fusion.36
  353.4 6.4 constant_dynamic-update-slice_fusion.34
  401.3 6.4 constant_dynamic-update-slice_fusion.41
  414.0 6.4 constant_dynamic-update-slice_fusion.39
  460.8 6.4 constant_dynamic-update-slice_fusion.46
  467.2 6.3 constant_dynamic-update-slice_fusion.45
  473.5 6.4 constant_dynamic-update-slice_fusion.44
  498.4 18.4 %all-to-all-start = ((f32[64,4,8]{2,1,0:T(4,128)}), f32[64,4,8]{2,1,0:T(4,128)S(1)}, u32[]{:S(2)}, u32[]{:S(2)}) async-start(f32[64,4,8]{2,1,0:T(4,128)} %copy.48), calls=%async_computation | async-start | bytes 262144 | tf_op jit(solution)/shard_map/all_to_all | solution.py:119
  516.8 17.0 %fusion = (f32[256,4,512]{2,1,0:T(4,128)}, f32[256,4,512]{2,1,0:T(4,128)}) fusion(f32[256,512]{1,0:T(8,128)S(1)} %mul.7300, f32[4]{0:T(128)S(1)} %add_multiply_fusion, f32[256,512]{1,0:T(8,128)S(1)} %mul.7297, f32[256,512]{1,0:T(8,128)S(1)} %neg.11), kind=kLoop, calls=%fused_computation.28 | loop fusion | flops 1572864 | bytes 5767184 | tf_op jit(solution)/shard_map/mul | solution.py:79
  546.9 96.8 %psum.7 = f32[2,4,512]{2,1,0:T(4,128)S(1)} all-reduce(f32[2,4,512]{2,1,0:T(4,128)S(1)} %pad_maximum_fusion.62), channel_id=1, replica_groups=mesh['axial'=64,'radial'=8] {'axial','radial'}, use_global_device_ids=true, to_apply=%region_0.3 | all-reduce | flops 4096 | bytes 32768 | tf_op jit(solution)/shard_map/psum | solution.py:127
  651.4 7.6 all-to-all-start.1
  659.1 10.0 all-to-all-done.1
  685.1 8.0 collective-permute-done.34
  711.3 6.5 constant_dynamic-update-slice_fusion.57
  717.8 6.4 constant_dynamic-update-slice_fusion.56
  770.7 6.5 constant_dynamic-update-slice_fusion.62
  777.2 6.4 constant_dynamic-update-slice_fusion.61
  829.8 6.5 constant_dynamic-update-slice_fusion.67
  836.3 6.4 constant_dynamic-update-slice_fusion.66
  887.9 6.5 constant_dynamic-update-slice_fusion.72
  894.4 6.4 constant_dynamic-update-slice_fusion.71
  945.6 6.5 constant_dynamic-update-slice_fusion.77
  952.2 6.4 constant_dynamic-update-slice_fusion.76
  1003.3 6.5 constant_dynamic-update-slice_fusion.82
  1009.8 6.4 constant_dynamic-update-slice_fusion.81
  1062.0 6.5 constant_dynamic-update-slice_fusion.87
  1068.5 6.4 constant_dynamic-update-slice_fusion.86
  1074.9 11.2 bitcast_add_fusion
  1100.5 7.3 collective-permute-done.62
  1125.9 6.5 constant_dynamic-update-slice_fusion.92
  1132.4 6.4 constant_dynamic-update-slice_fusion.91
  (408 shorter events, 708.5 us)
Async XLA Ops:
  1.8 10.9 collective-permute-start
  3.7 9.1 collective-permute-start.1
  12.9 14.0 %collective-permute-start.3 = (f32[5,20,5,128]{3,2,1,0:T(8,128)S(1)}, f32[5,20,5,128]{3,2,1,0:T(8,128)S(1)}, u32[]{:S(2)}, u32[]{:S(2)}) collective-permute-start(f32[5,20,5,128]{3,2,1,0:T(8,128)S(1)} %get-tuple-element.337), channel_id=1, source_target_pairs={{1,0},{2,1},{3,2},{4,3},{5,4},{6,5},{7,6},{9,8},{10,9},{11,10},{12... | collective-permute-start | bytes 768008 | tf_op jit(solution)/shard_map/ppermute | solution.py:25
  14.2 13.9 %collective-permute-start.2 = (f32[5,20,5,128]{3,2,1,0:T(8,128)S(1)}, f32[5,20,5,128]{3,2,1,0:T(8,128)S(1)}, u32[]{:S(2)}, u32[]{:S(2)}) collective-permute-start(f32[5,20,5,128]{3,2,1,0:T(8,128)S(1)} %get-tuple-element.338), channel_id=1, source_target_pairs={{0,1},{1,2},{2,3},{3,4},{4,5},{5,6},{6,7},{8,9},{9,10},{10,11},{11... | collective-permute-start | bytes 768008 | tf_op jit(solution)/shard_map/ppermute | solution.py:22
  62.1 7.4 collective-permute-start.4
  64.0 7.2 collective-permute-start.5
  71.3 12.8 %collective-permute-start.6 = (f32[5,20,5,128]{3,2,1,0:T(8,128)S(1)}, f32[5,20,5,128]{3,2,1,0:T(8,128)S(1)}, u32[]{:S(2)}, u32[]{:S(2)}) collective-permute-start(f32[5,20,5,128]{3,2,1,0:T(8,128)S(1)} %get-tuple-element.335), channel_id=1, source_target_pairs={{0,1},{1,2},{2,3},{3,4},{4,5},{5,6},{6,7},{8,9},{9,10},{10,11},{11... | collective-permute-start | bytes 768008 | tf_op jit(solution)/shard_map/ppermute | solution.py:22
  75.7 13.1 %collective-permute-start.7 = (f32[5,20,5,128]{3,2,1,0:T(8,128)S(1)}, f32[5,20,5,128]{3,2,1,0:T(8,128)S(1)}, u32[]{:S(2)}, u32[]{:S(2)}) collective-permute-start(f32[5,20,5,128]{3,2,1,0:T(8,128)S(1)} %get-tuple-element.336), channel_id=1, source_target_pairs={{1,0},{2,1},{3,2},{4,3},{5,4},{6,5},{7,6},{9,8},{10,9},{11,10},{12... | collective-permute-start | bytes 768008 | tf_op jit(solution)/shard_map/ppermute | solution.py:25
  122.8 7.1 collective-permute-start.8
  131.7 9.5 collective-permute-start.10
  134.4 12.6 %collective-permute-start.11 = (f32[5,20,5,128]{3,2,1,0:T(8,128)S(1)}, f32[5,20,5,128]{3,2,1,0:T(8,128)S(1)}, u32[]{:S(2)}, u32[]{:S(2)}) collective-permute-start(f32[5,20,5,128]{3,2,1,0:T(8,128)S(1)} %get-tuple-element.332), channel_id=1, source_target_pairs={{1,0},{2,1},{3,2},{4,3},{5,4},{6,5},{7,6},{9,8},{10,9},{11,10},{12... | collective-permute-start | bytes 768008 | tf_op jit(solution)/shard_map/ppermute | solution.py:25
  181.5 14.0 %collective-permute-start.12 = (f32[5,5,16,128]{3,2,1,0:T(8,128)}, f32[5,5,16,128]{3,2,1,0:T(8,128)S(1)}, u32[]{:S(2)}, u32[]{:S(2)}) collective-permute-start(f32[5,5,16,128]{3,2,1,0:T(8,128)} %get-tuple-element.363), channel_id=1, source_target_pairs={{0,8},{8,16},{16,24},{24,32},{32,40},{40,48},{48,56},{56,64},{64,7... | collective-permute-start | bytes 614408 | tf_op jit(solution)/shard_map/ppermute | solution.py:22
  186.2 9.2 collective-permute-start.13
  195.6 12.9 %collective-permute-start.14 = (f32[5,20,5,128]{3,2,1,0:T(8,128)S(1)}, f32[5,20,5,128]{3,2,1,0:T(8,128)S(1)}, u32[]{:S(2)}, u32[]{:S(2)}) collective-permute-start(f32[5,20,5,128]{3,2,1,0:T(8,128)S(1)} %get-tuple-element.327), channel_id=1, source_target_pairs={{0,1},{1,2},{2,3},{3,4},{4,5},{5,6},{6,7},{8,9},{9,10},{10,11},{11... | collective-permute-start | bytes 768008 | tf_op jit(solution)/shard_map/ppermute | solution.py:22
  201.0 12.4 %collective-permute-start.15 = (f32[5,20,5,128]{3,2,1,0:T(8,128)S(1)}, f32[5,20,5,128]{3,2,1,0:T(8,128)S(1)}, u32[]{:S(2)}, u32[]{:S(2)}) collective-permute-start(f32[5,20,5,128]{3,2,1,0:T(8,128)S(1)} %get-tuple-element.328), channel_id=1, source_target_pairs={{1,0},{2,1},{3,2},{4,3},{5,4},{6,5},{7,6},{9,8},{10,9},{11,10},{12... | collective-permute-start | bytes 768008 | tf_op jit(solution)/shard_map/ppermute | solution.py:25
  247.9 12.4 %collective-permute-start.16 = (f32[5,5,16,128]{3,2,1,0:T(8,128)}, f32[5,5,16,128]{3,2,1,0:T(8,128)S(1)}, u32[]{:S(2)}, u32[]{:S(2)}) collective-permute-start(f32[5,5,16,128]{3,2,1,0:T(8,128)} %get-tuple-element.361), channel_id=1, source_target_pairs={{0,8},{8,16},{16,24},{24,32},{32,40},{40,48},{48,56},{56,64},{64,7... | collective-permute-start | bytes 614408 | tf_op jit(solution)/shard_map/ppermute | solution.py:22
  251.7 8.6 collective-permute-start.17
  261.2 12.9 %collective-permute-start.18 = (f32[5,20,5,128]{3,2,1,0:T(8,128)}, f32[5,20,5,128]{3,2,1,0:T(8,128)}, u32[]{:S(2)}, u32[]{:S(2)}) collective-permute-start(f32[5,20,5,128]{3,2,1,0:T(8,128)} %get-tuple-element.323), channel_id=1, source_target_pairs={{0,1},{1,2},{2,3},{3,4},{4,5},{5,6},{6,7},{8,9},{9,10},{10,11},{11... | collective-permute-start | bytes 768008 | tf_op jit(solution)/shard_map/ppermute | solution.py:22
  266.1 13.4 %collective-permute-start.19 = (f32[5,20,5,128]{3,2,1,0:T(8,128)S(1)}, f32[5,20,5,128]{3,2,1,0:T(8,128)}, u32[]{:S(2)}, u32[]{:S(2)}) collective-permute-start(f32[5,20,5,128]{3,2,1,0:T(8,128)S(1)} %get-tuple-element.324), channel_id=1, source_target_pairs={{1,0},{2,1},{3,2},{4,3},{5,4},{6,5},{7,6},{9,8},{10,9},{11,10},{12... | collective-permute-start | bytes 768008 | tf_op jit(solution)/shard_map/ppermute | solution.py:25
  314.1 8.0 collective-permute-start.20
  323.8 9.2 collective-permute-start.22
  326.3 12.0 %collective-permute-start.23 = (f32[5,20,5,128]{3,2,1,0:T(8,128)S(1)}, f32[5,20,5,128]{3,2,1,0:T(8,128)}, u32[]{:S(2)}, u32[]{:S(2)}) collective-permute-start(f32[5,20,5,128]{3,2,1,0:T(8,128)S(1)} %get-tuple-element.320), channel_id=1, source_target_pairs={{1,0},{2,1},{3,2},{4,3},{5,4},{6,5},{7,6},{9,8},{10,9},{11,10},{12... | collective-permute-start | bytes 768008 | tf_op jit(solution)/shard_map/ppermute | solution.py:25
  373.0 8.5 collective-permute-start.24
  383.6 9.8 collective-permute-start.26
  387.4 11.5 %collective-permute-start.27 = (f32[5,20,5,128]{3,2,1,0:T(8,128)S(1)}, f32[5,20,5,128]{3,2,1,0:T(8,128)}, u32[]{:S(2)}, u32[]{:S(2)}) collective-permute-start(f32[5,20,5,128]{3,2,1,0:T(8,128)S(1)} %get-tuple-element.316), channel_id=1, source_target_pairs={{1,0},{2,1},{3,2},{4,3},{5,4},{6,5},{7,6},{9,8},{10,9},{11,10},{12... | collective-permute-start | bytes 768008 | tf_op jit(solution)/shard_map/ppermute | solution.py:25
  433.6 9.2 collective-permute-start.28
  445.5 9.3 collective-permute-start.30
  448.3 11.2 collective-permute-start.31
  498.4 40.4 %all-to-all-start = ((f32[64,4,8]{2,1,0:T(4,128)}), f32[64,4,8]{2,1,0:T(4,128)S(1)}, u32[]{:S(2)}, u32[]{:S(2)}) async-start(f32[64,4,8]{2,1,0:T(4,128)} %copy.48), calls=%async_computation | async-start | bytes 262144 | tf_op jit(solution)/shard_map/all_to_all | solution.py:119
  651.4 17.7 %all-to-all-start.1 = ((f32[64,4,8]{2,1,0:T(4,128)}), f32[64,4,8]{2,1,0:T(4,128)S(1)}, u32[]{:S(2)}, u32[]{:S(2)}) async-start(f32[64,4,8]{2,1,0:T(4,128)} %bitcast.105), calls=%async_computation.1 | async-start | bytes 262144 | tf_op jit(solution)/shard_map/all_to_all | solution.py:130
  672.3 7.7 collective-permute-start.32
  681.3 11.8 %collective-permute-start.34 = (f32[5,20,5,128]{3,2,1,0:T(8,128)S(1)}, f32[5,20,5,128]{3,2,1,0:T(8,128)S(1)}, u32[]{:S(2)}, u32[]{:S(2)}) collective-permute-start(f32[5,20,5,128]{3,2,1,0:T(8,128)S(1)} %get-tuple-element.307), channel_id=1, source_target_pairs={{0,1},{1,2},{2,3},{3,4},{4,5},{5,6},{6,7},{8,9},{9,10},{10,11},{11... | collective-permute-start | bytes 768008 | tf_op jit(solution)/shard_map/ppermute | solution.py:22
  683.4 14.0 %collective-permute-start.35 = (f32[5,20,5,128]{3,2,1,0:T(8,128)S(1)}, f32[5,20,5,128]{3,2,1,0:T(8,128)S(1)}, u32[]{:S(2)}, u32[]{:S(2)}) collective-permute-start(f32[5,20,5,128]{3,2,1,0:T(8,128)S(1)} %get-tuple-element.308), channel_id=1, source_target_pairs={{1,0},{2,1},{3,2},{4,3},{5,4},{6,5},{7,6},{9,8},{10,9},{11,10},{12... | collective-permute-start | bytes 768008 | tf_op jit(solution)/shard_map/ppermute | solution.py:25
  730.4 7.1 collective-permute-start.36
  739.3 13.0 %collective-permute-start.38 = (f32[5,20,5,128]{3,2,1,0:T(8,128)S(1)}, f32[5,20,5,128]{3,2,1,0:T(8,128)S(1)}, u32[]{:S(2)}, u32[]{:S(2)}) collective-permute-start(f32[5,20,5,128]{3,2,1,0:T(8,128)S(1)} %get-tuple-element.303), channel_id=1, source_target_pairs={{0,1},{1,2},{2,3},{3,4},{4,5},{5,6},{6,7},{8,9},{9,10},{10,11},{11... | collective-permute-start | bytes 768008 | tf_op jit(solution)/shard_map/ppermute | solution.py:22
  742.6 14.2 %collective-permute-start.39 = (f32[5,20,5,128]{3,2,1,0:T(8,128)S(1)}, f32[5,20,5,128]{3,2,1,0:T(8,128)S(1)}, u32[]{:S(2)}, u32[]{:S(2)}) collective-permute-start(f32[5,20,5,128]{3,2,1,0:T(8,128)S(1)} %get-tuple-element.304), channel_id=1, source_target_pairs={{1,0},{2,1},{3,2},{4,3},{5,4},{6,5},{7,6},{9,8},{10,9},{11,10},{12... | collective-permute-start | bytes 768008 | tf_op jit(solution)/shard_map/ppermute | solution.py:25
  798.8 13.1 %collective-permute-start.42 = (f32[5,20,5,128]{3,2,1,0:T(8,128)S(1)}, f32[5,20,5,128]{3,2,1,0:T(8,128)S(1)}, u32[]{:S(2)}, u32[]{:S(2)}) collective-permute-start(f32[5,20,5,128]{3,2,1,0:T(8,128)S(1)} %get-tuple-element.299), channel_id=1, source_target_pairs={{0,1},{1,2},{2,3},{3,4},{4,5},{5,6},{6,7},{8,9},{9,10},{10,11},{11... | collective-permute-start | bytes 768008 | tf_op jit(solution)/shard_map/ppermute | solution.py:22
  802.5 13.4 %collective-permute-start.43 = (f32[5,20,5,128]{3,2,1,0:T(8,128)S(1)}, f32[5,20,5,128]{3,2,1,0:T(8,128)S(1)}, u32[]{:S(2)}, u32[]{:S(2)}) collective-permute-start(f32[5,20,5,128]{3,2,1,0:T(8,128)S(1)} %get-tuple-element.300), channel_id=1, source_target_pairs={{1,0},{2,1},{3,2},{4,3},{5,4},{6,5},{7,6},{9,8},{10,9},{11,10},{12... | collective-permute-start | bytes 768008 | tf_op jit(solution)/shard_map/ppermute | solution.py:25
  857.9 12.0 %collective-permute-start.46 = (f32[5,20,5,128]{3,2,1,0:T(8,128)S(1)}, f32[5,20,5,128]{3,2,1,0:T(8,128)S(1)}, u32[]{:S(2)}, u32[]{:S(2)}) collective-permute-start(f32[5,20,5,128]{3,2,1,0:T(8,128)S(1)} %get-tuple-element.295), channel_id=1, source_target_pairs={{0,1},{1,2},{2,3},{3,4},{4,5},{5,6},{6,7},{8,9},{9,10},{10,11},{11... | collective-permute-start | bytes 768008 | tf_op jit(solution)/shard_map/ppermute | solution.py:22
  861.6 12.5 %collective-permute-start.47 = (f32[5,20,5,128]{3,2,1,0:T(8,128)S(1)}, f32[5,20,5,128]{3,2,1,0:T(8,128)S(1)}, u32[]{:S(2)}, u32[]{:S(2)}) collective-permute-start(f32[5,20,5,128]{3,2,1,0:T(8,128)S(1)} %get-tuple-element.296), channel_id=1, source_target_pairs={{1,0},{2,1},{3,2},{4,3},{5,4},{6,5},{7,6},{9,8},{10,9},{11,10},{12... | collective-permute-start | bytes 768008 | tf_op jit(solution)/shard_map/ppermute | solution.py:25
  916.0 11.6 %collective-permute-start.50 = (f32[5,20,5,128]{3,2,1,0:T(8,128)S(1)}, f32[5,20,5,128]{3,2,1,0:T(8,128)S(1)}, u32[]{:S(2)}, u32[]{:S(2)}) collective-permute-start(f32[5,20,5,128]{3,2,1,0:T(8,128)S(1)} %get-tuple-element.291), channel_id=1, source_target_pairs={{0,1},{1,2},{2,3},{3,4},{4,5},{5,6},{6,7},{8,9},{9,10},{10,11},{11... | collective-permute-start | bytes 768008 | tf_op jit(solution)/shard_map/ppermute | solution.py:22
  919.5 12.3 %collective-permute-start.51 = (f32[5,20,5,128]{3,2,1,0:T(8,128)S(1)}, f32[5,20,5,128]{3,2,1,0:T(8,128)S(1)}, u32[]{:S(2)}, u32[]{:S(2)}) collective-permute-start(f32[5,20,5,128]{3,2,1,0:T(8,128)S(1)} %get-tuple-element.292), channel_id=1, source_target_pairs={{1,0},{2,1},{3,2},{4,3},{5,4},{6,5},{7,6},{9,8},{10,9},{11,10},{12... | collective-permute-start | bytes 768008 | tf_op jit(solution)/shard_map/ppermute | solution.py:25
  973.7 11.6 %collective-permute-start.54 = (f32[5,20,5,128]{3,2,1,0:T(8,128)S(1)}, f32[5,20,5,128]{3,2,1,0:T(8,128)S(1)}, u32[]{:S(2)}, u32[]{:S(2)}) collective-permute-start(f32[5,20,5,128]{3,2,1,0:T(8,128)S(1)} %get-tuple-element.287), channel_id=1, source_target_pairs={{0,1},{1,2},{2,3},{3,4},{4,5},{5,6},{6,7},{8,9},{9,10},{10,11},{11... | collective-permute-start | bytes 768008 | tf_op jit(solution)/shard_map/ppermute | solution.py:22
  976.9 12.5 %collective-permute-start.55 = (f32[5,20,5,128]{3,2,1,0:T(8,128)S(1)}, f32[5,20,5,128]{3,2,1,0:T(8,128)S(1)}, u32[]{:S(2)}, u32[]{:S(2)}) collective-permute-start(f32[5,20,5,128]{3,2,1,0:T(8,128)S(1)} %get-tuple-element.288), channel_id=1, source_target_pairs={{1,0},{2,1},{3,2},{4,3},{5,4},{6,5},{7,6},{9,8},{10,9},{11,10},{12... | collective-permute-start | bytes 768008 | tf_op jit(solution)/shard_map/ppermute | solution.py:25
  1031.4 12.6 %collective-permute-start.58 = (f32[5,20,5,128]{3,2,1,0:T(8,128)S(1)}, f32[5,20,5,128]{3,2,1,0:T(8,128)S(1)}, u32[]{:S(2)}, u32[]{:S(2)}) collective-permute-start(f32[5,20,5,128]{3,2,1,0:T(8,128)S(1)} %get-tuple-element.283), channel_id=1, source_target_pairs={{0,1},{1,2},{2,3},{3,4},{4,5},{5,6},{6,7},{8,9},{9,10},{10,11},{11... | collective-permute-start | bytes 768008 | tf_op jit(solution)/shard_map/ppermute | solution.py:22
  1034.6 13.5 %collective-permute-start.59 = (f32[5,20,5,128]{3,2,1,0:T(8,128)S(1)}, f32[5,20,5,128]{3,2,1,0:T(8,128)S(1)}, u32[]{:S(2)}, u32[]{:S(2)}) collective-permute-start(f32[5,20,5,128]{3,2,1,0:T(8,128)S(1)} %get-tuple-element.284), channel_id=1, source_target_pairs={{1,0},{2,1},{3,2},{4,3},{5,4},{6,5},{7,6},{9,8},{10,9},{11,10},{12... | collective-permute-start | bytes 768008 | tf_op jit(solution)/shard_map/ppermute | solution.py:25
  1095.1 12.8 %collective-permute-start.62 = (f32[5,20,5,128]{3,2,1,0:T(8,128)S(1)}, f32[5,20,5,128]{3,2,1,0:T(8,128)S(1)}, u32[]{:S(2)}, u32[]{:S(2)}) collective-permute-start(f32[5,20,5,128]{3,2,1,0:T(8,128)S(1)} %get-tuple-element.279), channel_id=1, source_target_pairs={{0,1},{1,2},{2,3},{3,4},{4,5},{5,6},{6,7},{8,9},{9,10},{10,11},{11... | collective-permute-start | bytes 768008 | tf_op jit(solution)/shard_map/ppermute | solution.py:22
  1098.3 13.7 %collective-permute-start.63 = (f32[5,20,5,128]{3,2,1,0:T(8,128)S(1)}, f32[5,20,5,128]{3,2,1,0:T(8,128)S(1)}, u32[]{:S(2)}, u32[]{:S(2)}) collective-permute-start(f32[5,20,5,128]{3,2,1,0:T(8,128)S(1)} %get-tuple-element.280), channel_id=1, source_target_pairs={{1,0},{2,1},{3,2},{4,3},{5,4},{6,5},{7,6},{9,8},{10,9},{11,10},{12... | collective-permute-start | bytes 768008 | tf_op jit(solution)/shard_map/ppermute | solution.py:25
  (30 other events, 226.2 us)
where the time goes:
time: 1160 us; the launch traced here: 1150 us
  other arithmetic  585 us (50%)
  waiting for transfers between devices  200 us (17%)
  starting transfers between devices  196 us (17%)
  blocking collectives  96.8 us (8%)
  local copies, waits for them, and re-layouts  49.8 us (4%)
  matrix products  14.5 us (1%)
    unnamed x71, other arithmetic  411 us
    ppermute x32, starting transfers between devices, extended(): lax.ppermute(lax.slice_in_dim(block, block.shape[dim] - width, None, axis...  99.1 us
    ppermute x32, waiting for transfers between devices, extended(): lax.ppermute(lax.slice_in_dim(block, 0, width, axis=dim), axis, backward)  98.5 us
    psum x1, blocking collectives, on_device(): total = lax.psum(partial_sum, ('axial', 'radial'))  96.8 us
    another operation x15, other arithmetic, advance(): return jnp.stack(outputs)  92.6 us
    ppermute x32, waiting for transfers between devices, extended(): lax.ppermute(lax.slice_in_dim(block, block.shape[dim] - width, None, axis...  91.8 us
    ppermute x32, starting transfers between devices, extended(): lax.ppermute(lax.slice_in_dim(block, 0, width, axis=dim), axis, backward)  71 us
  transfers between devices with their start and end apart: 66, of which 55 were waited for; matrix products, arithmetic and copies ran while one was open for 7% of the time, Pallas kernels for 0%

commit v1 on v0

--- a/solution.py
+++ b/solution.py
@@ -124,7 +124,7 @@
     cos_t, sin_t = time_tables()
     partial_sum = partial_spectra(received.reshape(-1, STEPS), kern_re, kern_im, cos_t, sin_t)
     share = observers // lax.axis_size(("axial", "radial"))
-    total = lax.psum(partial_sum, ("axial", "radial"))
+    total = jnp.sum(lax.all_gather(partial_sum, ("axial", "radial")), axis=0)
     mine = lax.dynamic_slice_in_dim(total, lax.axis_index(("axial", "radial")) * share, share, 2)
     sources = panel_sources(total, kern_re, kern_im, cos_t, sin_t).reshape(received.shape)
     returned = lax.all_to_all(sources, "axial", split_axis=0, concat_axis=0, tiled=True)

time: 1160 us -> 1210 us (1.043)
  the two profiles are of different devices: /device:TPU:64 before, /device:TPU:2 now
where the time goes in v1:
time: 1210 us; the launch traced here: 1190 us
  other arithmetic  586 us (48%)
  waiting for transfers between devices  286 us (24%)
  starting transfers between devices  237 us (20%)
  local copies, waits for them, and re-layouts  49.9 us (4%)
  between operations  16.6 us (1%)
  matrix products  14.5 us (1%)
    unnamed x71, other arithmetic  403 us
    ppermute x32, starting transfers between devices, extended(): lax.ppermute(lax.slice_in_dim(block, 0, width, axis=dim), axis, backward)  125 us
    all_gather x1, waiting for transfers between devices, on_device(): total = jnp.sum(lax.all_gather(partial_sum, ('axial', 'radial')), axis=0)  124 us
    another operation x15, other arithmetic, advance(): return jnp.stack(outputs)  95.9 us
    ppermute x32, starting transfers between devices, extended(): lax.ppermute(lax.slice_in_dim(block, block.shape[dim] - width, None, axis...  91.2 us
    ppermute x32, waiting for transfers between devices, extended(): lax.ppermute(lax.slice_in_dim(block, 0, width, axis=dim), axis, backward)  90 us
    ppermute x32, waiting for transfers between devices, extended(): lax.ppermute(lax.slice_in_dim(block, block.shape[dim] - width, None, axis...  62.6 us
  transfers between devices with their start and end apart: 67, of which 56 were waited for; matrix products, arithmetic and copies ran while one was open for 6% of the time, Pallas kernels for 0%

profile of v1, /device:TPU:2, one launch (start us, length us, event | category | flops | bytes accessed | tf_op | source)
XLA Modules:
  0.0 1189.7 jit_solution(3566010077796977237)
XLA Ops:
  10.2 10.4 collective-permute-start.1
  39.1 6.3 constant_dynamic-update-slice_fusion.11
  45.3 6.3 constant_dynamic-update-slice_fusion.10
  64.1 6.4 constant_dynamic-update-slice_fusion.7
  99.2 6.3 constant_dynamic-update-slice_fusion.16
  105.5 6.3 constant_dynamic-update-slice_fusion.15
  124.2 6.4 constant_dynamic-update-slice_fusion.12
  133.2 8.0 collective-permute-start.9
  166.9 6.3 constant_dynamic-update-slice_fusion.20
  185.6 6.4 constant_dynamic-update-slice_fusion.17
  195.3 7.7 collective-permute-start.13
  233.8 6.3 constant_dynamic-update-slice_fusion.25
  252.5 6.5 constant_dynamic-update-slice_fusion.22
  292.9 6.3 constant_dynamic-update-slice_fusion.31
  299.1 6.3 constant_dynamic-update-slice_fusion.30
  317.8 6.4 constant_dynamic-update-slice_fusion.27
  358.6 6.3 constant_dynamic-update-slice_fusion.35
  377.3 6.4 constant_dynamic-update-slice_fusion.32
  386.3 7.9 collective-permute-start.25
  414.1 6.3 constant_dynamic-update-slice_fusion.41
  420.3 6.3 constant_dynamic-update-slice_fusion.40
  439.0 6.4 constant_dynamic-update-slice_fusion.37
  448.0 7.1 collective-permute-start.29
  472.5 6.3 constant_dynamic-update-slice_fusion.46
  478.8 6.3 constant_dynamic-update-slice_fusion.45
  497.5 6.4 constant_dynamic-update-slice_fusion.42
  509.8 12.0 %all-to-all-start = ((f32[64,4,8]{2,1,0:T(4,128)}), f32[64,4,8]{2,1,0:T(4,128)S(1)}, u32[]{:S(2)}, u32[]{:S(2)}) async-start(f32[64,4,8]{2,1,0:T(4,128)} %copy.64), calls=%async_computation | async-start | bytes 262144 | tf_op jit(solution)/shard_map/all_to_all | solution.py:119
  521.9 17.0 %fusion = (f32[256,4,512]{2,1,0:T(4,128)}, f32[256,4,512]{2,1,0:T(4,128)}) fusion(f32[256,512]{1,0:T(8,128)S(1)} %mul.7300, f32[4]{0:T(128)S(1)} %add_multiply_fusion, f32[256,512]{1,0:T(8,128)S(1)} %mul.7297, f32[256,512]{1,0:T(8,128)S(1)} %neg.11), kind=kLoop, calls=%fused_computation.28 | loop fusion | flops 1572864 | bytes 5767184 | tf_op jit(solution)/shard_map/mul | solution.py:79
  552.9 123.6 %all-gather.3.cloned.1.call-done = f32[1024,4,512]{2,1,0:T(4,128)} async-done(((f32[2,4,512]{2,1,0:T(4,128)}), f32[1024,4,512]{2,1,0:T(4,128)}) %all-gather.3.cloned.1.call-update) | async-done | bytes 8388624 | tf_op jit(solution)/shard_map/all_gather | solution.py:127
  688.7 8.7 all-to-all-start.1
  697.4 9.4 all-to-all-done.1
  725.7 6.8 collective-permute-done.34
  738.0 6.3 constant_dynamic-update-slice_fusion.59
  762.9 6.4 constant_dynamic-update-slice_fusion.55
  796.8 6.3 constant_dynamic-update-slice_fusion.64
  821.7 6.4 constant_dynamic-update-slice_fusion.60
  856.8 6.3 constant_dynamic-update-slice_fusion.69
  881.7 6.4 constant_dynamic-update-slice_fusion.65
  915.6 6.3 constant_dynamic-update-slice_fusion.74
  940.6 6.4 constant_dynamic-update-slice_fusion.70
  973.8 6.3 constant_dynamic-update-slice_fusion.79
  998.7 6.4 constant_dynamic-update-slice_fusion.75
  1031.1 6.3 constant_dynamic-update-slice_fusion.84
  1056.0 6.4 constant_dynamic-update-slice_fusion.80
  1088.4 6.3 constant_dynamic-update-slice_fusion.89
  1113.3 11.5 bitcast_add_fusion
  1150.6 6.3 constant_dynamic-update-slice_fusion.94
  1175.5 6.4 constant_dynamic-update-slice_fusion.90
  (411 shorter events, 715.0 us)
Async XLA Ops:
  8.3 17.6 %collective-permute-start = (f32[5,5,16,128]{3,2,1,0:T(8,128)S(1)}, f32[5,5,16,128]{3,2,1,0:T(8,128)S(1)}, u32[]{:S(2)}, u32[]{:S(2)}) collective-permute-start(f32[5,5,16,128]{3,2,1,0:T(8,128)S(1)} %get-tuple-element.372), channel_id=1, source_target_pairs={{0,8},{8,16},{16,24},{24,32},{32,40},{40,48},{48,56},{56,64},{64,7... | collective-permute-start | bytes 614408 | tf_op jit(solution)/shard_map/ppermute | solution.py:22
  10.2 15.8 %collective-permute-start.1 = (f32[5,5,16,128]{3,2,1,0:T(8,128)S(1)}, f32[5,5,16,128]{3,2,1,0:T(8,128)S(1)}, u32[]{:S(2)}, u32[]{:S(2)}) collective-permute-start(f32[5,5,16,128]{3,2,1,0:T(8,128)S(1)} %get-tuple-element.373), channel_id=1, source_target_pairs={{8,0},{16,8},{24,16},{32,24},{40,32},{48,40},{56,48},{64,56},{72,6... | collective-permute-start | bytes 614408 | tf_op jit(solution)/shard_map/ppermute | solution.py:25
  26.2 9.8 collective-permute-start.3
  27.5 10.0 collective-permute-start.2
  82.3 11.3 collective-permute-start.6
  86.7 11.0 collective-permute-start.7
  131.3 11.4 collective-permute-start.8
  133.2 11.2 collective-permute-start.9
  148.1 11.2 collective-permute-start.11
  193.4 16.9 %collective-permute-start.12 = (f32[5,5,16,128]{3,2,1,0:T(8,128)}, f32[5,5,16,128]{3,2,1,0:T(8,128)S(1)}, u32[]{:S(2)}, u32[]{:S(2)}) collective-permute-start(f32[5,5,16,128]{3,2,1,0:T(8,128)} %get-tuple-element.363), channel_id=1, source_target_pairs={{0,8},{8,16},{16,24},{24,32},{32,40},{40,48},{48,56},{56,64},{64,7... | collective-permute-start | bytes 614408 | tf_op jit(solution)/shard_map/ppermute | solution.py:22
  195.3 15.0 %collective-permute-start.13 = (f32[5,5,16,128]{3,2,1,0:T(8,128)}, f32[5,5,16,128]{3,2,1,0:T(8,128)S(1)}, u32[]{:S(2)}, u32[]{:S(2)}) collective-permute-start(f32[5,5,16,128]{3,2,1,0:T(8,128)} %get-tuple-element.364), channel_id=1, source_target_pairs={{8,0},{16,8},{24,16},{32,24},{40,32},{48,40},{56,48},{64,56},{72,6... | collective-permute-start | bytes 614408 | tf_op jit(solution)/shard_map/ppermute | solution.py:25
  210.5 10.8 collective-permute-start.14
  216.3 9.8 collective-permute-start.15
  260.5 14.4 %collective-permute-start.16 = (f32[5,5,16,128]{3,2,1,0:T(8,128)}, f32[5,5,16,128]{3,2,1,0:T(8,128)S(1)}, u32[]{:S(2)}, u32[]{:S(2)}) collective-permute-start(f32[5,5,16,128]{3,2,1,0:T(8,128)} %get-tuple-element.361), channel_id=1, source_target_pairs={{0,8},{8,16},{16,24},{24,32},{32,40},{40,48},{48,56},{56,64},{64,7... | collective-permute-start | bytes 614408 | tf_op jit(solution)/shard_map/ppermute | solution.py:22
  262.4 12.5 %collective-permute-start.17 = (f32[5,5,16,128]{3,2,1,0:T(8,128)}, f32[5,5,16,128]{3,2,1,0:T(8,128)S(1)}, u32[]{:S(2)}, u32[]{:S(2)}) collective-permute-start(f32[5,5,16,128]{3,2,1,0:T(8,128)} %get-tuple-element.362), channel_id=1, source_target_pairs={{8,0},{16,8},{24,16},{32,24},{40,32},{48,40},{56,48},{64,56},{72,6... | collective-permute-start | bytes 614408 | tf_op jit(solution)/shard_map/ppermute | solution.py:25
  275.8 9.7 collective-permute-start.18
  280.4 9.9 collective-permute-start.19
  325.0 10.1 collective-permute-start.20
  339.9 9.9 collective-permute-start.23
  384.4 12.3 %collective-permute-start.24 = (f32[5,5,16,128]{3,2,1,0:T(8,128)S(1)}, f32[5,5,16,128]{3,2,1,0:T(8,128)S(1)}, u32[]{:S(2)}, u32[]{:S(2)}) collective-permute-start(f32[5,5,16,128]{3,2,1,0:T(8,128)S(1)} %get-tuple-element.357), channel_id=1, source_target_pairs={{0,8},{8,16},{16,24},{24,32},{32,40},{40,48},{48,56},{56,64},{64,7... | collective-permute-start | bytes 614408 | tf_op jit(solution)/shard_map/ppermute | solution.py:22
  386.3 11.2 collective-permute-start.25
  401.6 9.9 collective-permute-start.27
  446.1 11.5 collective-permute-start.28
  448.0 10.3 collective-permute-start.29
  461.4 9.8 collective-permute-start.31
  509.8 34.1 %all-to-all-start = ((f32[64,4,8]{2,1,0:T(4,128)}), f32[64,4,8]{2,1,0:T(4,128)S(1)}, u32[]{:S(2)}, u32[]{:S(2)}) async-start(f32[64,4,8]{2,1,0:T(4,128)} %copy.64), calls=%async_computation | async-start | bytes 262144 | tf_op jit(solution)/shard_map/all_to_all | solution.py:119
  521.9 154.6 %all-gather.3.cloned.1.call-start = ((), (), s32[]{:S(2)}) async-start(), calls=%async_computation.2 | async-start | bytes 8404992 | tf_op jit(solution)/shard_map/all_gather | solution.py:127
  688.7 18.1 %all-to-all-start.1 = ((f32[64,4,8]{2,1,0:T(4,128)}), f32[64,4,8]{2,1,0:T(4,128)S(1)}, u32[]{:S(2)}, u32[]{:S(2)}) async-start(f32[64,4,8]{2,1,0:T(4,128)} %bitcast.106), calls=%async_computation.1 | async-start | bytes 262144 | tf_op jit(solution)/shard_map/all_to_all | solution.py:130
  710.0 9.8 collective-permute-start.32
  721.1 11.5 collective-permute-start.34
  724.2 12.5 %collective-permute-start.35 = (f32[5,20,5,128]{3,2,1,0:T(8,128)S(1)}, f32[5,20,5,128]{3,2,1,0:T(8,128)S(1)}, u32[]{:S(2)}, u32[]{:S(2)}) collective-permute-start(f32[5,20,5,128]{3,2,1,0:T(8,128)S(1)} %get-tuple-element.308), channel_id=1, source_target_pairs={{1,0},{2,1},{3,2},{4,3},{5,4},{6,5},{7,6},{9,8},{10,9},{11,10},{12... | collective-permute-start | bytes 768008 | tf_op jit(solution)/shard_map/ppermute | solution.py:25
  769.4 9.2 collective-permute-start.36
  780.5 10.8 collective-permute-start.38
  783.5 11.9 %collective-permute-start.39 = (f32[5,20,5,128]{3,2,1,0:T(8,128)S(1)}, f32[5,20,5,128]{3,2,1,0:T(8,128)S(1)}, u32[]{:S(2)}, u32[]{:S(2)}) collective-permute-start(f32[5,20,5,128]{3,2,1,0:T(8,128)S(1)} %get-tuple-element.304), channel_id=1, source_target_pairs={{1,0},{2,1},{3,2},{4,3},{5,4},{6,5},{7,6},{9,8},{10,9},{11,10},{12... | collective-permute-start | bytes 768008 | tf_op jit(solution)/shard_map/ppermute | solution.py:25
  828.2 9.2 collective-permute-start.40
  839.2 11.9 %collective-permute-start.42 = (f32[5,20,5,128]{3,2,1,0:T(8,128)S(1)}, f32[5,20,5,128]{3,2,1,0:T(8,128)S(1)}, u32[]{:S(2)}, u32[]{:S(2)}) collective-permute-start(f32[5,20,5,128]{3,2,1,0:T(8,128)S(1)} %get-tuple-element.299), channel_id=1, source_target_pairs={{0,1},{1,2},{2,3},{3,4},{4,5},{5,6},{6,7},{8,9},{9,10},{10,11},{11... | collective-permute-start | bytes 768008 | tf_op jit(solution)/shard_map/ppermute | solution.py:22
  843.6 11.9 collective-permute-start.43
  899.3 10.9 collective-permute-start.46
  902.9 11.3 collective-permute-start.47
  947.0 9.2 collective-permute-start.48
  958.1 10.2 collective-permute-start.50
  961.5 11.0 collective-permute-start.51
  1005.2 9.2 collective-permute-start.52
  1016.3 9.4 collective-permute-start.54
  1019.8 9.9 collective-permute-start.55
  1062.5 9.2 collective-permute-start.56
  1077.2 9.8 collective-permute-start.59
  1139.4 9.8 collective-permute-start.63
  (31 other events, 295.1 us)
Sparse Core Ops, SparseCore 0:
  552.9 123.5 all-gather.2
